TPU v7x, 256 devices: a whole 4x4x8 slice. The times are simulated.
256 devices in a mesh: pipe: 8 (over z), seq: 16 (over x, y), tp: 2 (over core).
Axes of the slice: x: 4, y: 4, z: 8, core: 2. Of those that a mesh axis runs over, the one named last changes fastest.
Arguments:
- layer_inputs: bfloat16 [8, 2048, 4096], P('pipe', ('seq', 'tp')), may hold values from -6 to 6
- out_grad: bfloat16 [2048, 4096], P('seq', 'tp'), may hold values from -6 to 6
- short_weights: bfloat16 [8, 7, 3, 4096], P('pipe', None, None, 'tp'), may hold values from -2 to 2
- long_filters: bfloat16 [8, 256, 128], P('pipe', 'tp'), may hold values from -0.15625 to 0.15625
- out_weights: bfloat16 [8, 4096, 4096], P('pipe', 'tp', 'seq'), may hold values from -0.09375 to 0.09375
Outputs:
- input_grad: bfloat16 [8, 2048, 4096], P('pipe', 'seq', 'tp')
- short_grad: float32 [8, 7, 3, 4096], P('pipe', None, None, 'tp')
- long_grad: float32 [8, 256, 128], P('pipe', 'tp')
All inputs are finite; a program needn't handle non-finite values.
Results may differ from a plain program's by a relative error of at most 0.03.
Values may be sent and summed in bfloat16 or wider, within the bound.
No kernel may reach another device: no remote copies, remote signals or barrier semaphores. Data moves between devices by JAX's collectives and lax.ppermute only.
A program may use at most 192 MiB of HBM per device.

v0:
```python
import jax
import jax.numpy as jnp
from jax import lax
from jax.sharding import PartitionSpec as P


def passed_along(array, axis, by):
    size = lax.axis_size(axis)
    pairs = [(i, i + by) for i in range(size) if 0 <= i + by < size]
    return lax.ppermute(array, axis, pairs)


def toeplitz_blocks(filters):
    groups, kernel_width = filters.shape
    base_row = jnp.concatenate(
        [
            jnp.zeros((groups, 1), filters.dtype),
            filters[:, ::-1],
            jnp.zeros((groups, kernel_width), filters.dtype),
        ],
        axis=1,
    )
    tiled = jnp.tile(base_row, (1, kernel_width))[:, : 2 * kernel_width * kernel_width]
    return tiled.reshape(groups, kernel_width, 2 * kernel_width)


def lag_sums(products):
    groups, kernel_width, window = products.shape
    flattened = products.reshape(groups, kernel_width * window)
    flattened = jnp.pad(flattened, ((0, 0), (0, kernel_width)))
    skewed = flattened.reshape(groups, kernel_width, window + 1)
    totals = jnp.sum(skewed, axis=1)
    return totals[:, 1 : kernel_width + 1][:, ::-1]


def to_groups(rows, groups):
    count = rows.shape[0]
    return jnp.transpose(rows.reshape(count, groups, rows.shape[1] // groups), (1, 2, 0))


def from_groups(blocks):
    groups, width, count = blocks.shape
    return jnp.transpose(blocks, (2, 0, 1)).reshape(count, groups * width)


def featurize(source, weights):
    tap_count = weights.shape[0]
    row_count = source.shape[0] - tap_count + 1
    running = jnp.zeros((weights.shape[1], row_count, source.shape[1]), jnp.float32)
    for offset in range(tap_count):
        start = tap_count - 1 - offset
        running = running + weights[offset][:, None, :] * source[start : start + row_count][None]
    return running


def spread_back(feature_grads, weights):
    tap_count = weights.shape[0]
    row_count = feature_grads.shape[1] - tap_count + 1
    running = jnp.zeros((row_count, feature_grads.shape[2]), jnp.float32)
    for offset in range(tap_count):
        running = running + jnp.sum(
            weights[offset][:, None, :] * feature_grads[:, offset : offset + row_count], axis=0
        )
    return running


def weight_grads(feature_grads, source):
    row_count = feature_grads.shape[1]
    tap_count = source.shape[0] - row_count + 1
    terms = []
    for offset in range(tap_count):
        start = tap_count - 1 - offset
        terms.append(jnp.sum(feature_grads * source[start : start + row_count][None], axis=1))
    return jnp.stack(terms)


def long_forward(padded, toeplitz, groups):
    grouped = to_groups(padded, groups)
    result = jnp.einsum("gis,gcs->gci", toeplitz, grouped, preferred_element_type=jnp.float32)
    return from_groups(result)


def long_backward(trailing, reversed_band, groups):
    grouped = to_groups(trailing, groups)
    result = jnp.einsum("grj,gcr->gcj", reversed_band, grouped, preferred_element_type=jnp.float32)
    return from_groups(result)


def filter_grads(mixed_grad, padded, groups):
    grad_groups = to_groups(mixed_grad, groups)
    value_groups = to_groups(padded, groups)
    products = jnp.einsum(
        "gci,gcs->gis", grad_groups, value_groups, preferred_element_type=jnp.float32
    )
    return lag_sums(products)


def recompute(layer_block, weights, filters):
    local_rows = lax.all_to_all(layer_block, "tp", split_axis=1, concat_axis=0, tiled=True)
    tap_count = weights.shape[0]
    kernel_width = filters.shape[1]
    before = passed_along(local_rows[local_rows.shape[0] - tap_count + 1 :], "seq", 1)
    extended = jnp.concatenate([before, local_rows], axis=0).astype(jnp.float32)
    features = featurize(extended, weights)
    products = (features[1] * features[2]).astype(jnp.bfloat16)
    earlier_products = passed_along(products[products.shape[0] - kernel_width + 1 :], "seq", 1)
    padded = jnp.concatenate(
        [jnp.zeros((1, products.shape[1]), jnp.bfloat16), earlier_products, products], axis=0
    )
    toeplitz = toeplitz_blocks(filters)
    reversed_band = jnp.concatenate(
        [toeplitz[:, :, kernel_width:], toeplitz[:, :, :kernel_width]], axis=1
    )
    mixed_rows = long_forward(padded, toeplitz, filters.shape[0])
    return (features, padded, reversed_band, mixed_rows, extended)


def dense_grad(incoming, columns, active):
    empty_sum = jnp.zeros((incoming.shape[0], columns.shape[0]), jnp.float32)
    piece = lax.all_gather(incoming, "tp", axis=1, tiled=True)
    summed = lax.cond(
        active,
        lambda: jnp.einsum("td,cd->tc", piece, columns, preferred_element_type=jnp.float32),
        lambda: empty_sum,
    )
    return summed.astype(jnp.bfloat16)


def backward(saved_state, incoming, dense_part, weights, groups, active):
    features, padded, reversed_band, mixed_rows, source = saved_state
    tap_count = weights.shape[0]
    kernel_width = reversed_band.shape[2]
    token_count, channels = incoming.shape
    edge_rows = tap_count - 1
    dense_float = dense_part.astype(jnp.float32)
    mixed_grad = (dense_float * features[0]).astype(jnp.bfloat16)
    after_grad = passed_along(mixed_grad[: kernel_width - 1], "seq", -1)
    trailing_grad = jnp.concatenate(
        [mixed_grad, after_grad, jnp.zeros((1, channels), jnp.bfloat16)], axis=0
    )

    def middle(operand):
        product_grad = long_backward(operand, reversed_band, groups)
        query_grad = dense_float * mixed_rows
        return (
            jnp.stack([query_grad, product_grad * features[2], product_grad * features[1]]),
            product_grad,
        )

    def middle_skipped(operand):
        return (
            jnp.zeros((3, token_count, channels), jnp.float32),
            jnp.zeros((token_count, channels), jnp.float32),
        )

    feature_grads, product_grad = lax.cond(active, middle, middle_skipped, trailing_grad)
    head_zeros = jnp.zeros((3, edge_rows, channels), jnp.float32)
    partial_sums = spread_back(
        jnp.concatenate([head_zeros, feature_grads[:, :edge_rows]], axis=1), weights
    )
    overflow = passed_along(partial_sums.astype(jnp.bfloat16), "seq", -1).astype(partial_sums.dtype)

    def finish(operands):
        grads, spill = operands
        trailing = jnp.concatenate([grads, head_zeros], axis=1)
        tail_rows = jnp.concatenate(
            [jnp.zeros((token_count - edge_rows, channels), jnp.float32), spill], axis=0
        )
        total = incoming.astype(jnp.float32) + spread_back(trailing, weights) + tail_rows
        return total.astype(jnp.bfloat16)

    def finish_skipped(operands):
        return jnp.zeros((token_count, channels), jnp.bfloat16)

    return (lax.cond(active, finish, finish_skipped, (feature_grads, overflow)), product_grad)


def per_device(layer_inputs, out_grad, short_weights, long_filters, out_weights):
    sections = lax.axis_size("pipe")
    section_index = lax.axis_index("pipe")
    weights = short_weights[0].astype(jnp.float32)
    filters = long_filters[0]
    groups = filters.shape[0]
    saved_state = recompute(layer_inputs[0], weights, filters)
    features, padded, reversed_band, mixed_rows, source = saved_state
    columns = lax.all_gather(out_weights[0], "seq", axis=1, tiled=True)
    incoming = out_grad
    input_result = jnp.zeros_like(out_grad)
    dense_kept = jnp.zeros(out_grad.shape, jnp.bfloat16)
    product_kept = jnp.zeros(out_grad.shape, jnp.float32)
    for step_index in range(sections):
        active = section_index == sections - 1 - step_index
        dense_part = dense_grad(incoming, columns, active)
        input_grad, product_grad = backward(
            saved_state, incoming, dense_part, weights, groups, active
        )
        input_result = jnp.where(active, input_grad, input_result)
        dense_kept = jnp.where(active, dense_part, dense_kept)
        product_kept = jnp.where(active, product_grad, product_kept)
        if step_index + 1 < sections:
            incoming = passed_along(input_grad, "pipe", -1)
    dense_float = dense_kept.astype(jnp.float32)
    mixed_grad = (dense_float * features[0]).astype(jnp.bfloat16)
    feature_grads = jnp.stack(
        [dense_float * mixed_rows, product_kept * features[2], product_kept * features[1]]
    )
    short_local = weight_grads(feature_grads, source)
    long_local = filter_grads(mixed_grad, padded, groups)
    short_result, long_result = (
        lax.psum(short_local.astype(jnp.bfloat16), "seq").astype(jnp.float32),
        lax.psum(long_local.astype(jnp.bfloat16), "seq").astype(jnp.float32),
    )
    return (input_result[None], short_result[None], long_result[None])


def solution(mesh):
    in_specs = (
        P("pipe", ("seq", "tp"), None),
        P("seq", "tp"),
        P("pipe", None, None, "tp"),
        P("pipe", "tp", None),
        P("pipe", "tp", "seq"),
    )
    out_specs = (P("pipe", "seq", "tp"), P("pipe", None, None, "tp"), P("pipe", "tp", None))
    return jax.shard_map(
        per_device, mesh=mesh, in_specs=in_specs, out_specs=out_specs, check_vma=False
    )
```

profile of v0, /device:TPU:32, one launch (start us, length us, event | category | flops | bytes accessed | tf_op | source)
XLA Modules:
  0.0 1389.2 jit_solution(17497464794075836733)
XLA Ops:
  22.8 13.0 tile.10
  42.9 12.5 copy.273
  88.4 68.1 %all-gather.27.cloned.1.call-done = bf16[1,2048,4096]{2,1,0:T(8,128)(2,1)} async-done(((bf16[1,2048,256]{2,1,0:T(8,128)(2,1)}), bf16[1,2048,4096]{2,1,0:T(8,128)(2,1)}) %all-gather.27.cloned.1.call-update) | async-done | bytes 16777232 | tf_op jit(solution)/shard_map/all_gather | solution.py:186
  235.9 56.1 %all-gather.13.cloned.1.call-done = bf16[128,4096]{1,0:T(8,128)(2,1)} async-done(((bf16[128,2048]{1,0:T(8,128)(2,1)}), bf16[128,4096]{1,0:T(8,128)(2,1)}) %all-gather.13.cloned.1.call-update) | async-done | bytes 1048592 | tf_op jit(solution)/shard_map/all_gather | solution.py:120
  298.1 14.7 %collective-permute-done.5 = bf16[127,2048]{0,1:T(8,128)(2,1)S(1)} collective-permute-done((bf16[127,2048]{0,1:T(8,128)(2,1)S(1)}, bf16[127,2048]{0,1:T(8,128)(2,1)S(1)}, u32[]{:S(2)}, u32[]{:S(2)}) %collective-permute-start.5) | collective-permute-done | bytes 520224 | tf_op jit(solution)/shard_map/ppermute | solution.py:10
  330.3 13.9 %collective-permute-done.6 = bf16[6,2048]{0,1:T(8,128)(2,1)S(1)} collective-permute-done((bf16[6,2048]{0,1:T(8,128)(2,1)S(1)}, bf16[6,2048]{0,1:T(8,128)(2,1)S(1)}, u32[]{:S(2)}, u32[]{:S(2)}) %collective-permute-start.6) | collective-permute-done | bytes 24608 | tf_op jit(solution)/shard_map/ppermute | solution.py:10
  361.0 63.3 %all-gather.15.cloned.1.call-done = bf16[128,4096]{1,0:T(8,128)(2,1)} async-done(((bf16[128,2048]{1,0:T(8,128)(2,1)}), bf16[128,4096]{1,0:T(8,128)(2,1)}) %all-gather.15.cloned.1.call-update) | async-done | bytes 1048592 | tf_op jit(solution)/shard_map/all_gather | solution.py:120
  430.1 14.7 %collective-permute-done.8 = bf16[127,2048]{0,1:T(8,128)(2,1)S(1)} collective-permute-done((bf16[127,2048]{0,1:T(8,128)(2,1)S(1)}, bf16[127,2048]{0,1:T(8,128)(2,1)S(1)}, u32[]{:S(2)}, u32[]{:S(2)}) %collective-permute-start.8) | collective-permute-done | bytes 520224 | tf_op jit(solution)/shard_map/ppermute | solution.py:10
  462.6 13.9 %collective-permute-done.9 = bf16[6,2048]{0,1:T(8,128)(2,1)S(1)} collective-permute-done((bf16[6,2048]{0,1:T(8,128)(2,1)S(1)}, bf16[6,2048]{0,1:T(8,128)(2,1)S(1)}, u32[]{:S(2)}, u32[]{:S(2)}) %collective-permute-start.9) | collective-permute-done | bytes 24608 | tf_op jit(solution)/shard_map/ppermute | solution.py:10
  493.1 64.1 %all-gather.17.cloned.1.call-done = bf16[128,4096]{1,0:T(8,128)(2,1)} async-done(((bf16[128,2048]{1,0:T(8,128)(2,1)}), bf16[128,4096]{1,0:T(8,128)(2,1)}) %all-gather.17.cloned.1.call-update) | async-done | bytes 1048592 | tf_op jit(solution)/shard_map/all_gather | solution.py:120
  562.9 14.7 %collective-permute-done.11 = bf16[127,2048]{0,1:T(8,128)(2,1)S(1)} collective-permute-done((bf16[127,2048]{0,1:T(8,128)(2,1)S(1)}, bf16[127,2048]{0,1:T(8,128)(2,1)S(1)}, u32[]{:S(2)}, u32[]{:S(2)}) %collective-permute-start.11) | collective-permute-done | bytes 520224 | tf_op jit(solution)/shard_map/ppermute | solution.py:10
  595.6 13.9 %collective-permute-done.12 = bf16[6,2048]{0,1:T(8,128)(2,1)S(1)} collective-permute-done((bf16[6,2048]{0,1:T(8,128)(2,1)S(1)}, bf16[6,2048]{0,1:T(8,128)(2,1)S(1)}, u32[]{:S(2)}, u32[]{:S(2)}) %collective-permute-start.12) | collective-permute-done | bytes 24608 | tf_op jit(solution)/shard_map/ppermute | solution.py:10
  626.1 65.0 %all-gather.19.cloned.1.call-done = bf16[128,4096]{1,0:T(8,128)(2,1)} async-done(((bf16[128,2048]{1,0:T(8,128)(2,1)}), bf16[128,4096]{1,0:T(8,128)(2,1)}) %all-gather.19.cloned.1.call-update) | async-done | bytes 1048592 | tf_op jit(solution)/shard_map/all_gather | solution.py:120
  696.9 14.7 %collective-permute-done.14 = bf16[127,2048]{0,1:T(8,128)(2,1)S(1)} collective-permute-done((bf16[127,2048]{0,1:T(8,128)(2,1)S(1)}, bf16[127,2048]{0,1:T(8,128)(2,1)S(1)}, u32[]{:S(2)}, u32[]{:S(2)}) %collective-permute-start.14) | collective-permute-done | bytes 520224 | tf_op jit(solution)/shard_map/ppermute | solution.py:10
  729.2 13.9 %collective-permute-done.15 = bf16[6,2048]{0,1:T(8,128)(2,1)S(1)} collective-permute-done((bf16[6,2048]{0,1:T(8,128)(2,1)S(1)}, bf16[6,2048]{0,1:T(8,128)(2,1)S(1)}, u32[]{:S(2)}, u32[]{:S(2)}) %collective-permute-start.15) | collective-permute-done | bytes 24608 | tf_op jit(solution)/shard_map/ppermute | solution.py:10
  759.9 64.0 %all-gather.21.cloned.1.call-done = bf16[128,4096]{1,0:T(8,128)(2,1)} async-done(((bf16[128,2048]{1,0:T(8,128)(2,1)}), bf16[128,4096]{1,0:T(8,128)(2,1)}) %all-gather.21.cloned.1.call-update) | async-done | bytes 1048592 | tf_op jit(solution)/shard_map/all_gather | solution.py:120
  829.6 14.7 %collective-permute-done.17 = bf16[127,2048]{0,1:T(8,128)(2,1)S(1)} collective-permute-done((bf16[127,2048]{0,1:T(8,128)(2,1)S(1)}, bf16[127,2048]{0,1:T(8,128)(2,1)S(1)}, u32[]{:S(2)}, u32[]{:S(2)}) %collective-permute-start.17) | collective-permute-done | bytes 520224 | tf_op jit(solution)/shard_map/ppermute | solution.py:10
  862.3 13.9 %collective-permute-done.18 = bf16[6,2048]{0,1:T(8,128)(2,1)S(1)} collective-permute-done((bf16[6,2048]{0,1:T(8,128)(2,1)S(1)}, bf16[6,2048]{0,1:T(8,128)(2,1)S(1)}, u32[]{:S(2)}, u32[]{:S(2)}) %collective-permute-start.18) | collective-permute-done | bytes 24608 | tf_op jit(solution)/shard_map/ppermute | solution.py:10
  880.8 57.0 %collective-permute-done.19 = bf16[128,2048]{1,0:T(8,128)(2,1)} collective-permute-done((bf16[128,2048]{1,0:T(8,128)(2,1)}, bf16[128,2048]{1,0:T(8,128)(2,1)}, u32[]{:S(2)}, u32[]{:S(2)}) %collective-permute-start.19) | collective-permute-done | bytes 524320 | tf_op jit(solution)/shard_map/ppermute | solution.py:10
  937.8 16.7 %all-gather.23.cloned.1.call-done = bf16[128,4096]{1,0:T(8,128)(2,1)} async-done(((bf16[128,2048]{1,0:T(8,128)(2,1)}), bf16[128,4096]{1,0:T(8,128)(2,1)}) %all-gather.23.cloned.1.call-update) | async-done | bytes 1048592 | tf_op jit(solution)/shard_map/all_gather | solution.py:120
  954.5 17.2 %conditional.42 = (f32[128,2048]{1,0:T(8,128)}, f32[128,2048]{0,1:T(8,128)}, bf16[128,2048]{0,1:T(8,128)(2,1)}) conditional(s32[]{:T(128)} %convert_element_type.283, () %tuple.255, (bf16[128,4096]{1,0:T(8,128)(2,1)}, bf16[2048,4096]{1,0:T(8,128)(2,1)}) %tuple.637), branch_computations={%region_115.116_spmd, %region_116.117_spmd} | conditional | flops 2148007936 | bytes 22020120 | solution.py:121
  954.5 12.9 fusion.9
  974.4 14.7 %collective-permute-done.20 = bf16[127,2048]{0,1:T(8,128)(2,1)S(1)} collective-permute-done((bf16[127,2048]{0,1:T(8,128)(2,1)S(1)}, bf16[127,2048]{0,1:T(8,128)(2,1)S(1)}, u32[]{:S(2)}, u32[]{:S(2)}) %collective-permute-start.20) | collective-permute-done | bytes 520224 | tf_op jit(solution)/shard_map/ppermute | solution.py:10
  990.5 13.2 conditional.43
  1017.9 13.9 %collective-permute-done.21 = bf16[6,2048]{0,1:T(8,128)(2,1)S(1)} collective-permute-done((bf16[6,2048]{0,1:T(8,128)(2,1)S(1)}, bf16[6,2048]{0,1:T(8,128)(2,1)S(1)}, u32[]{:S(2)}, u32[]{:S(2)}) %collective-permute-start.21) | collective-permute-done | bytes 24608 | tf_op jit(solution)/shard_map/ppermute | solution.py:10
  1032.9 20.9 %conditional.44 = (bf16[128,2048]{1,0:T(8,128)(2,1)}) conditional(s32[]{:T(128)} %convert_element_type.283, () %tuple.217, (bf16[128,2048]{1,0:T(8,128)(2,1)}, f32[7,3,2048]{2,1,0:T(4,128)S(1)}, f32[3,128,2048]{1,2,0:T(8,128)}, f32[6,2048]{0,1:T(8,128)}) %tuple.258), branch_computations={%region_125.126_spmd, %region_126.134_spmd} | conditional | flops 11796480 | bytes 26026020 | solution.py:175
  1055.7 12.7 collective-permute-done.22
  1099.4 17.8 %copy.274 = f32[128,128,256]{0,2,1:T(8,128)} copy(f32[128,128,256]{2,1,0:T(8,128)} %fusion.30) | data formatting | bytes 33554432 | tf_op jit(solution)/shard_map/reshape | solution.py:29
  1117.2 13.3 pad.28
  1130.5 17.5 %reshape.203 = f32[128,128,257]{0,2,1:T(8,128)} reshape(f32[128,32896]{0,1:T(8,128)} %pad.28) | data formatting | bytes 33685504 | tf_op jit(solution)/shard_map/reshape | solution.py:31
  1158.1 77.1 %psum.15 = bf16[1,128,128]{1,2,0:T(8,128)(2,1)} all-reduce(bf16[1,128,128]{1,2,0:T(8,128)(2,1)} %bitcast.399), channel_id=1, replica_groups=mesh['pipe'=8,'seq'=16,'tp'=2] {'seq'}, use_global_device_ids=true, to_apply=%region_162.163 | all-reduce | flops 16384 | bytes 65536 | tf_op jit(solution)/shard_map/psum | solution.py:211
  1280.5 99.8 %all-reduce.27.cloned.1.call-done = bf16[1,7,3,2048]{3,1,2,0:T(8,128)(2,1)} async-done(((bf16[1,7,3,2048]{3,1,2,0:T(8,128)(2,1)}), bf16[1,7,3,2048]{3,1,2,0:T(8,128)(2,1)}) %all-reduce.27.cloned.1.call-update) | async-done | bytes 86032 | tf_op jit(solution)/shard_map/psum | solution.py:210
  (299 shorter events, 513.0 us)
Async XLA Ops:
  7.2 81.3 %all-gather.11.cloned.1.call-start = ((), (), s32[]{:S(2)}) async-start(), calls=%async_computation.1 | async-start | bytes 1572864 | tf_op jit(solution)/shard_map/all_gather | solution.py:120
  7.9 148.7 %all-gather.27.cloned.1.call-start = ((), (), s32[]{:S(2)}) async-start(), calls=%async_computation.10 | async-start | bytes 17825792 | tf_op jit(solution)/shard_map/all_gather | solution.py:186
  8.7 283.3 %all-gather.13.cloned.1.call-start = ((), (), s32[]{:S(2)}) async-start(), calls=%async_computation.2 | async-start | bytes 1572864 | tf_op jit(solution)/shard_map/all_gather | solution.py:120
  14.5 47.9 %collective-permute-start = (bf16[6,2048]{1,0:T(8,128)(2,1)S(1)}, bf16[6,2048]{1,0:T(8,128)(2,1)S(1)}, u32[]{:S(2)}, u32[]{:S(2)}) collective-permute-start(bf16[6,2048]{1,0:T(8,128)(2,1)S(1)} %slice.757), channel_id=1, source_target_pairs={{0,2},{2,4},{4,6},{6,8},{8,10},{10,12},{12,14},{14,16},{16,18},{18... | collective-permute-start | bytes 73736 | tf_op jit(solution)/shard_map/ppermute | solution.py:10
  163.8 13.7 collective-permute-start.1
  167.7 14.7 %collective-permute-start.2 = (bf16[127,2048]{0,1:T(8,128)(2,1)}, bf16[127,2048]{0,1:T(8,128)(2,1)}, u32[]{:S(2)}, u32[]{:S(2)}) collective-permute-start(bf16[127,2048]{0,1:T(8,128)(2,1)} %bitcast.344), channel_id=1, source_target_pairs={{2,0},{4,2},{6,4},{8,6},{10,8},{12,10},{14,12},{16,14},{18,16},{20... | collective-permute-start | bytes 1560584 | tf_op jit(solution)/shard_map/ppermute | solution.py:10
  235.8 188.6 %all-gather.15.cloned.1.call-start = ((), (), s32[]{:S(2)}) async-start(), calls=%async_computation.3 | async-start | bytes 1572864 | tf_op jit(solution)/shard_map/all_gather | solution.py:120
  296.8 16.0 %collective-permute-start.5 = (bf16[127,2048]{0,1:T(8,128)(2,1)S(1)}, bf16[127,2048]{0,1:T(8,128)(2,1)S(1)}, u32[]{:S(2)}, u32[]{:S(2)}) collective-permute-start(bf16[127,2048]{0,1:T(8,128)(2,1)S(1)} %bitcast.392), channel_id=1, source_target_pairs={{2,0},{4,2},{6,4},{8,6},{10,8},{12,10},{14,12},{16,14},{18,16},{20... | collective-permute-start | bytes 1560584 | tf_op jit(solution)/shard_map/ppermute | solution.py:10
  329.0 15.2 %collective-permute-start.6 = (bf16[6,2048]{0,1:T(8,128)(2,1)S(1)}, bf16[6,2048]{0,1:T(8,128)(2,1)S(1)}, u32[]{:S(2)}, u32[]{:S(2)}) collective-permute-start(bf16[6,2048]{0,1:T(8,128)(2,1)S(1)} %add_convert_fusion.14), channel_id=1, source_target_pairs={{2,0},{4,2},{6,4},{8,6},{10,8},{12,10},{14,12},{16,14},{18,16},{20... | collective-permute-start | bytes 73736 | tf_op jit(solution)/shard_map/ppermute | solution.py:10
  346.4 14.6 %collective-permute-start.7 = (bf16[128,2048]{1,0:T(8,128)(2,1)}, bf16[128,2048]{1,0:T(8,128)(2,1)}, u32[]{:S(2)}, u32[]{:S(2)}) collective-permute-start(bf16[128,2048]{1,0:T(8,128)(2,1)} %get-tuple-element.1088), channel_id=1, source_target_pairs={{32,0},{64,32},{96,64},{128,96},{160,128},{192,160},{224,192},{33,... | collective-permute-start | bytes 1572872 | tf_op jit(solution)/shard_map/ppermute | solution.py:10
  361.0 196.2 %all-gather.17.cloned.1.call-start = ((), (), s32[]{:S(2)}) async-start(), calls=%async_computation.4 | async-start | bytes 1572864 | tf_op jit(solution)/shard_map/all_gather | solution.py:120
  428.8 16.0 %collective-permute-start.8 = (bf16[127,2048]{0,1:T(8,128)(2,1)S(1)}, bf16[127,2048]{0,1:T(8,128)(2,1)S(1)}, u32[]{:S(2)}, u32[]{:S(2)}) collective-permute-start(bf16[127,2048]{0,1:T(8,128)(2,1)S(1)} %bitcast.393), channel_id=1, source_target_pairs={{2,0},{4,2},{6,4},{8,6},{10,8},{12,10},{14,12},{16,14},{18,16},{20... | collective-permute-start | bytes 1560584 | tf_op jit(solution)/shard_map/ppermute | solution.py:10
  461.3 15.2 %collective-permute-start.9 = (bf16[6,2048]{0,1:T(8,128)(2,1)S(1)}, bf16[6,2048]{0,1:T(8,128)(2,1)S(1)}, u32[]{:S(2)}, u32[]{:S(2)}) collective-permute-start(bf16[6,2048]{0,1:T(8,128)(2,1)S(1)} %add_convert_fusion.13), channel_id=1, source_target_pairs={{2,0},{4,2},{6,4},{8,6},{10,8},{12,10},{14,12},{16,14},{18,16},{20... | collective-permute-start | bytes 73736 | tf_op jit(solution)/shard_map/ppermute | solution.py:10
  478.4 14.6 %collective-permute-start.10 = (bf16[128,2048]{1,0:T(8,128)(2,1)}, bf16[128,2048]{1,0:T(8,128)(2,1)}, u32[]{:S(2)}, u32[]{:S(2)}) collective-permute-start(bf16[128,2048]{1,0:T(8,128)(2,1)} %get-tuple-element.1089), channel_id=1, source_target_pairs={{32,0},{64,32},{96,64},{128,96},{160,128},{192,160},{224,192},{33,... | collective-permute-start | bytes 1572872 | tf_op jit(solution)/shard_map/ppermute | solution.py:10
  493.0 198.1 %all-gather.19.cloned.1.call-start = ((), (), s32[]{:S(2)}) async-start(), calls=%async_computation.5 | async-start | bytes 1572864 | tf_op jit(solution)/shard_map/all_gather | solution.py:120
  561.6 16.0 %collective-permute-start.11 = (bf16[127,2048]{0,1:T(8,128)(2,1)S(1)}, bf16[127,2048]{0,1:T(8,128)(2,1)S(1)}, u32[]{:S(2)}, u32[]{:S(2)}) collective-permute-start(bf16[127,2048]{0,1:T(8,128)(2,1)S(1)} %bitcast.394), channel_id=1, source_target_pairs={{2,0},{4,2},{6,4},{8,6},{10,8},{12,10},{14,12},{16,14},{18,16},{20... | collective-permute-start | bytes 1560584 | tf_op jit(solution)/shard_map/ppermute | solution.py:10
  594.3 15.2 %collective-permute-start.12 = (bf16[6,2048]{0,1:T(8,128)(2,1)S(1)}, bf16[6,2048]{0,1:T(8,128)(2,1)S(1)}, u32[]{:S(2)}, u32[]{:S(2)}) collective-permute-start(bf16[6,2048]{0,1:T(8,128)(2,1)S(1)} %add_convert_fusion.12), channel_id=1, source_target_pairs={{2,0},{4,2},{6,4},{8,6},{10,8},{12,10},{14,12},{16,14},{18,16},{20... | collective-permute-start | bytes 73736 | tf_op jit(solution)/shard_map/ppermute | solution.py:10
  611.4 14.6 %collective-permute-start.13 = (bf16[128,2048]{1,0:T(8,128)(2,1)}, bf16[128,2048]{1,0:T(8,128)(2,1)}, u32[]{:S(2)}, u32[]{:S(2)}) collective-permute-start(bf16[128,2048]{1,0:T(8,128)(2,1)} %get-tuple-element.1090), channel_id=1, source_target_pairs={{32,0},{64,32},{96,64},{128,96},{160,128},{192,160},{224,192},{33,... | collective-permute-start | bytes 1572872 | tf_op jit(solution)/shard_map/ppermute | solution.py:10
  626.1 197.9 %all-gather.21.cloned.1.call-start = ((), (), s32[]{:S(2)}) async-start(), calls=%async_computation.6 | async-start | bytes 1572864 | tf_op jit(solution)/shard_map/all_gather | solution.py:120
  695.6 16.0 %collective-permute-start.14 = (bf16[127,2048]{0,1:T(8,128)(2,1)S(1)}, bf16[127,2048]{0,1:T(8,128)(2,1)S(1)}, u32[]{:S(2)}, u32[]{:S(2)}) collective-permute-start(bf16[127,2048]{0,1:T(8,128)(2,1)S(1)} %bitcast.395), channel_id=1, source_target_pairs={{2,0},{4,2},{6,4},{8,6},{10,8},{12,10},{14,12},{16,14},{18,16},{20... | collective-permute-start | bytes 1560584 | tf_op jit(solution)/shard_map/ppermute | solution.py:10
  727.9 15.2 %collective-permute-start.15 = (bf16[6,2048]{0,1:T(8,128)(2,1)S(1)}, bf16[6,2048]{0,1:T(8,128)(2,1)S(1)}, u32[]{:S(2)}, u32[]{:S(2)}) collective-permute-start(bf16[6,2048]{0,1:T(8,128)(2,1)S(1)} %add_convert_fusion.11), channel_id=1, source_target_pairs={{2,0},{4,2},{6,4},{8,6},{10,8},{12,10},{14,12},{16,14},{18,16},{20... | collective-permute-start | bytes 73736 | tf_op jit(solution)/shard_map/ppermute | solution.py:10
  745.2 14.6 %collective-permute-start.16 = (bf16[128,2048]{1,0:T(8,128)(2,1)}, bf16[128,2048]{1,0:T(8,128)(2,1)}, u32[]{:S(2)}, u32[]{:S(2)}) collective-permute-start(bf16[128,2048]{1,0:T(8,128)(2,1)} %get-tuple-element.1091), channel_id=1, source_target_pairs={{32,0},{64,32},{96,64},{128,96},{160,128},{192,160},{224,192},{33,... | collective-permute-start | bytes 1572872 | tf_op jit(solution)/shard_map/ppermute | solution.py:10
  759.9 194.7 %all-gather.23.cloned.1.call-start = ((), (), s32[]{:S(2)}) async-start(), calls=%async_computation.7 | async-start | bytes 1572864 | tf_op jit(solution)/shard_map/all_gather | solution.py:120
  828.3 16.0 %collective-permute-start.17 = (bf16[127,2048]{0,1:T(8,128)(2,1)S(1)}, bf16[127,2048]{0,1:T(8,128)(2,1)S(1)}, u32[]{:S(2)}, u32[]{:S(2)}) collective-permute-start(bf16[127,2048]{0,1:T(8,128)(2,1)S(1)} %bitcast.396), channel_id=1, source_target_pairs={{2,0},{4,2},{6,4},{8,6},{10,8},{12,10},{14,12},{16,14},{18,16},{20... | collective-permute-start | bytes 1560584 | tf_op jit(solution)/shard_map/ppermute | solution.py:10
  861.0 15.2 %collective-permute-start.18 = (bf16[6,2048]{0,1:T(8,128)(2,1)S(1)}, bf16[6,2048]{0,1:T(8,128)(2,1)S(1)}, u32[]{:S(2)}, u32[]{:S(2)}) collective-permute-start(bf16[6,2048]{0,1:T(8,128)(2,1)S(1)} %add_convert_fusion.10), channel_id=1, source_target_pairs={{2,0},{4,2},{6,4},{8,6},{10,8},{12,10},{14,12},{16,14},{18,16},{20... | collective-permute-start | bytes 73736 | tf_op jit(solution)/shard_map/ppermute | solution.py:10
  878.1 59.6 %collective-permute-start.19 = (bf16[128,2048]{1,0:T(8,128)(2,1)}, bf16[128,2048]{1,0:T(8,128)(2,1)}, u32[]{:S(2)}, u32[]{:S(2)}) collective-permute-start(bf16[128,2048]{1,0:T(8,128)(2,1)} %get-tuple-element.1092), channel_id=1, source_target_pairs={{32,0},{64,32},{96,64},{128,96},{160,128},{192,160},{224,192},{33,... | collective-permute-start | bytes 1572872 | tf_op jit(solution)/shard_map/ppermute | solution.py:10
  937.8 146.2 %all-gather.25.cloned.1.call-start = ((), (), s32[]{:S(2)}) async-start(), calls=%async_computation.8 | async-start | bytes 1572864 | tf_op jit(solution)/shard_map/all_gather | solution.py:120
  973.1 16.0 %collective-permute-start.20 = (bf16[127,2048]{0,1:T(8,128)(2,1)S(1)}, bf16[127,2048]{0,1:T(8,128)(2,1)S(1)}, u32[]{:S(2)}, u32[]{:S(2)}) collective-permute-start(bf16[127,2048]{0,1:T(8,128)(2,1)S(1)} %bitcast.397), channel_id=1, source_target_pairs={{2,0},{4,2},{6,4},{8,6},{10,8},{12,10},{14,12},{16,14},{18,16},{20... | collective-permute-start | bytes 1560584 | tf_op jit(solution)/shard_map/ppermute | solution.py:10
  1016.6 15.2 %collective-permute-start.21 = (bf16[6,2048]{0,1:T(8,128)(2,1)S(1)}, bf16[6,2048]{0,1:T(8,128)(2,1)S(1)}, u32[]{:S(2)}, u32[]{:S(2)}) collective-permute-start(bf16[6,2048]{0,1:T(8,128)(2,1)S(1)} %add_convert_fusion.9), channel_id=1, source_target_pairs={{2,0},{4,2},{6,4},{8,6},{10,8},{12,10},{14,12},{16,14},{18,16},{20... | collective-permute-start | bytes 73736 | tf_op jit(solution)/shard_map/ppermute | solution.py:10
  1053.8 14.6 %collective-permute-start.22 = (bf16[128,2048]{1,0:T(8,128)(2,1)}, bf16[128,2048]{1,0:T(8,128)(2,1)}, u32[]{:S(2)}, u32[]{:S(2)}) collective-permute-start(bf16[128,2048]{1,0:T(8,128)(2,1)} %get-tuple-element.1093), channel_id=1, source_target_pairs={{32,0},{64,32},{96,64},{128,96},{160,128},{192,160},{224,192},{33,... | collective-permute-start | bytes 1572872 | tf_op jit(solution)/shard_map/ppermute | solution.py:10
  1068.4 311.9 %all-reduce.27.cloned.1.call-start = ((), (), s32[]{:S(2)}) async-start(), calls=%async_computation.9 | async-start | bytes 196608 | tf_op jit(solution)/shard_map/psum | solution.py:210
  1090.0 149.2 %collective-permute-start.23 = (bf16[127,2048]{0,1:T(8,128)(2,1)}, bf16[127,2048]{0,1:T(8,128)(2,1)}, u32[]{:S(2)}, u32[]{:S(2)}) collective-permute-start(bf16[127,2048]{0,1:T(8,128)(2,1)} %bitcast.351), channel_id=1, source_target_pairs={{2,0},{4,2},{6,4},{8,6},{10,8},{12,10},{14,12},{16,14},{18,16},{20... | collective-permute-start | bytes 1560584 | tf_op jit(solution)/shard_map/ppermute | solution.py:10
  (33 other events, 160.2 us)
Sparse Core Ops, SparseCore 0:
  9.8 16.9 all-gather.10
  29.2 127.3 all-gather.26
  235.9 55.9 all-gather.12
  361.1 63.2 all-gather.14
  493.1 63.9 all-gather.16
  626.2 64.8 all-gather.18
  760.0 63.8 all-gather.20
  937.9 16.6 all-gather.22
  1068.5 15.4 all-gather.24
  1268.5 111.7 all-reduce.26
where the time goes:
time: 1400 us; the launch traced here: 1390 us
  waiting for transfers between devices  826 us (59%)
  local copies, waits for them, and re-layouts  195 us (14%)
  other arithmetic  189 us (14%)
  blocking collectives  81.3 us (6%)
  starting transfers between devices  45.8 us (3%)
  matrix products  32.7 us (2%)
  between operations  15.6 us (1%)
    all_gather x8, waiting for transfers between devices, dense_grad(): piece = lax.all_gather(incoming, 'tp', axis=1, tiled=True)  330 us
    ppermute x25, waiting for transfers between devices, passed_along(): return lax.ppermute(array, axis, pairs)  327 us
    psum x1, waiting for transfers between devices, per_device(): lax.psum(short_local.astype(jnp.bfloat16), 'seq').astype(jnp.float32)  99.8 us
    reduce_sum x10, other arithmetic, spread_back(): jnp.sum(weights[offset][:, None, :] * feature_grads[:, offset:offset + ro...  88.6 us
    psum x1, blocking collectives, per_device(): lax.psum(long_local.astype(jnp.bfloat16), 'seq').astype(jnp.float32)  77.1 us
    all_gather x1, waiting for transfers between devices, per_device(): columns = lax.all_gather(out_weights[0], 'seq', axis=1, tiled=True)  68.1 us
    another operation x46, local copies, waits for them, and re-layouts  50.6 us
    ppermute x25, starting transfers between devices, passed_along(): return lax.ppermute(array, axis, pairs)  45.4 us
  transfers between devices with their start and end apart: 35, of which 32 were waited for; matrix products, arithmetic and copies ran while one was open for 12% of the time, Pallas kernels for 0%

commit v1 on v0

--- a/solution.py
+++ b/solution.py
@@ -1,7 +1,15 @@
+import functools
 import jax
 import jax.numpy as jnp
 from jax import lax
 from jax.sharding import PartitionSpec as P
+
+
+def _make_indices(vector, group_axis):
+    return lax.all_gather(vector, group_axis).sum(axis=0)
+
+
+list_cells_for = functools.partial(_make_indices, group_axis="seq")
 
 
 def passed_along(array, axis, by):
@@ -207,7 +215,7 @@
     short_local = weight_grads(feature_grads, source)
     long_local = filter_grads(mixed_grad, padded, groups)
     short_result, long_result = (
-        lax.psum(short_local.astype(jnp.bfloat16), "seq").astype(jnp.float32),
+        list_cells_for(short_local.astype(jnp.bfloat16)).astype(jnp.float32),
         lax.psum(long_local.astype(jnp.bfloat16), "seq").astype(jnp.float32),
     )
     return (input_result[None], short_result[None], long_result[None])

time: 1400 us -> 1340 us (0.957)
  the two profiles are of different devices: /device:TPU:32 before, /device:TPU:0 now
where the time goes in v1:
time: 1340 us; the launch traced here: 1330 us
  waiting for transfers between devices  791 us (59%)
  local copies, waits for them, and re-layouts  189 us (14%)
  other arithmetic  184 us (14%)
  blocking collectives  80.9 us (6%)
  starting transfers between devices  35.7 us (3%)
  matrix products  33.6 us (3%)
  between operations  15.7 us (1%)
    all_gather x8, waiting for transfers between devices, dense_grad(): piece = lax.all_gather(incoming, 'tp', axis=1, tiled=True)  395 us
    ppermute x25, waiting for transfers between devices, passed_along(): return lax.ppermute(array, axis, pairs)  327 us
    reduce_sum x10, other arithmetic, spread_back(): jnp.sum(weights[offset][:, None, :] * feature_grads[:, offset:offset + ro...  82 us
    psum x1, blocking collectives, per_device(): lax.psum(long_local.astype(jnp.bfloat16), 'seq').astype(jnp.float32)  76.7 us
    all_gather x1, waiting for transfers between devices, per_device(): columns = lax.all_gather(out_weights[0], 'seq', axis=1, tiled=True)  68 us
    another operation x46, local copies, waits for them, and re-layouts  46.8 us
    ppermute x25, starting transfers between devices, passed_along(): return lax.ppermute(array, axis, pairs)  35.3 us
  transfers between devices with their start and end apart: 35, of which 30 were waited for; matrix products, arithmetic and copies ran while one was open for 14% of the time, Pallas kernels for 0%

profile of v1, /device:TPU:0, one launch (start us, length us, event | category | flops | bytes accessed | tf_op | source)
XLA Modules:
  0.0 1332.4 jit_solution(16699903494795010281)
XLA Ops:
  87.2 68.0 %all-gather.30.cloned.1.call-done = bf16[1,2048,4096]{2,1,0:T(8,128)(2,1)} async-done(((bf16[1,2048,256]{2,1,0:T(8,128)(2,1)}), bf16[1,2048,4096]{2,1,0:T(8,128)(2,1)}) %all-gather.30.cloned.1.call-update) | async-done | bytes 16777232 | tf_op jit(solution)/shard_map/all_gather | solution.py:194
  234.5 56.9 %all-gather.14.cloned.1.call-done = bf16[128,4096]{1,0:T(8,128)(2,1)} async-done(((bf16[128,2048]{1,0:T(8,128)(2,1)}), bf16[128,4096]{1,0:T(8,128)(2,1)}) %all-gather.14.cloned.1.call-update) | async-done | bytes 1048592 | tf_op jit(solution)/shard_map/all_gather | solution.py:128
  297.5 14.7 %collective-permute-done.5 = bf16[127,2048]{0,1:T(8,128)(2,1)S(1)} collective-permute-done((bf16[127,2048]{0,1:T(8,128)(2,1)S(1)}, bf16[127,2048]{0,1:T(8,128)(2,1)S(1)}, u32[]{:S(2)}, u32[]{:S(2)}) %collective-permute-start.5) | collective-permute-done | bytes 520224 | tf_op jit(solution)/shard_map/ppermute | solution.py:18
  329.8 13.9 %collective-permute-done.6 = bf16[6,2048]{0,1:T(8,128)(2,1)S(1)} collective-permute-done((bf16[6,2048]{0,1:T(8,128)(2,1)S(1)}, bf16[6,2048]{0,1:T(8,128)(2,1)S(1)}, u32[]{:S(2)}, u32[]{:S(2)}) %collective-permute-start.6) | collective-permute-done | bytes 24608 | tf_op jit(solution)/shard_map/ppermute | solution.py:18
  347.2 13.3 collective-permute-done.7
  360.5 64.0 %all-gather.16.cloned.1.call-done = bf16[128,4096]{1,0:T(8,128)(2,1)} async-done(((bf16[128,2048]{1,0:T(8,128)(2,1)}), bf16[128,4096]{1,0:T(8,128)(2,1)}) %all-gather.16.cloned.1.call-update) | async-done | bytes 1048592 | tf_op jit(solution)/shard_map/all_gather | solution.py:128
  430.3 14.7 %collective-permute-done.8 = bf16[127,2048]{0,1:T(8,128)(2,1)S(1)} collective-permute-done((bf16[127,2048]{0,1:T(8,128)(2,1)S(1)}, bf16[127,2048]{0,1:T(8,128)(2,1)S(1)}, u32[]{:S(2)}, u32[]{:S(2)}) %collective-permute-start.8) | collective-permute-done | bytes 520224 | tf_op jit(solution)/shard_map/ppermute | solution.py:18
  462.8 13.9 %collective-permute-done.9 = bf16[6,2048]{0,1:T(8,128)(2,1)S(1)} collective-permute-done((bf16[6,2048]{0,1:T(8,128)(2,1)S(1)}, bf16[6,2048]{0,1:T(8,128)(2,1)S(1)}, u32[]{:S(2)}, u32[]{:S(2)}) %collective-permute-start.9) | collective-permute-done | bytes 24608 | tf_op jit(solution)/shard_map/ppermute | solution.py:18
  479.9 13.3 collective-permute-done.10
  493.3 64.9 %all-gather.18.cloned.1.call-done = bf16[128,4096]{1,0:T(8,128)(2,1)} async-done(((bf16[128,2048]{1,0:T(8,128)(2,1)}), bf16[128,4096]{1,0:T(8,128)(2,1)}) %all-gather.18.cloned.1.call-update) | async-done | bytes 1048592 | tf_op jit(solution)/shard_map/all_gather | solution.py:128
  563.8 14.7 %collective-permute-done.11 = bf16[127,2048]{0,1:T(8,128)(2,1)S(1)} collective-permute-done((bf16[127,2048]{0,1:T(8,128)(2,1)S(1)}, bf16[127,2048]{0,1:T(8,128)(2,1)S(1)}, u32[]{:S(2)}, u32[]{:S(2)}) %collective-permute-start.11) | collective-permute-done | bytes 520224 | tf_op jit(solution)/shard_map/ppermute | solution.py:18
  596.5 13.9 %collective-permute-done.12 = bf16[6,2048]{0,1:T(8,128)(2,1)S(1)} collective-permute-done((bf16[6,2048]{0,1:T(8,128)(2,1)S(1)}, bf16[6,2048]{0,1:T(8,128)(2,1)S(1)}, u32[]{:S(2)}, u32[]{:S(2)}) %collective-permute-start.12) | collective-permute-done | bytes 24608 | tf_op jit(solution)/shard_map/ppermute | solution.py:18
  613.7 13.3 collective-permute-done.13
  627.1 65.7 %all-gather.20.cloned.1.call-done = bf16[128,4096]{1,0:T(8,128)(2,1)} async-done(((bf16[128,2048]{1,0:T(8,128)(2,1)}), bf16[128,4096]{1,0:T(8,128)(2,1)}) %all-gather.20.cloned.1.call-update) | async-done | bytes 1048592 | tf_op jit(solution)/shard_map/all_gather | solution.py:128
  698.5 14.7 %collective-permute-done.14 = bf16[127,2048]{0,1:T(8,128)(2,1)S(1)} collective-permute-done((bf16[127,2048]{0,1:T(8,128)(2,1)S(1)}, bf16[127,2048]{0,1:T(8,128)(2,1)S(1)}, u32[]{:S(2)}, u32[]{:S(2)}) %collective-permute-start.14) | collective-permute-done | bytes 520224 | tf_op jit(solution)/shard_map/ppermute | solution.py:18
  730.9 13.9 %collective-permute-done.15 = bf16[6,2048]{0,1:T(8,128)(2,1)S(1)} collective-permute-done((bf16[6,2048]{0,1:T(8,128)(2,1)S(1)}, bf16[6,2048]{0,1:T(8,128)(2,1)S(1)}, u32[]{:S(2)}, u32[]{:S(2)}) %collective-permute-start.15) | collective-permute-done | bytes 24608 | tf_op jit(solution)/shard_map/ppermute | solution.py:18
  748.2 13.3 collective-permute-done.16
  761.6 64.6 %all-gather.22.cloned.1.call-done = bf16[128,4096]{1,0:T(8,128)(2,1)} async-done(((bf16[128,2048]{1,0:T(8,128)(2,1)}), bf16[128,4096]{1,0:T(8,128)(2,1)}) %all-gather.22.cloned.1.call-update) | async-done | bytes 1048592 | tf_op jit(solution)/shard_map/all_gather | solution.py:128
  831.9 14.7 %collective-permute-done.17 = bf16[127,2048]{0,1:T(8,128)(2,1)S(1)} collective-permute-done((bf16[127,2048]{0,1:T(8,128)(2,1)S(1)}, bf16[127,2048]{0,1:T(8,128)(2,1)S(1)}, u32[]{:S(2)}, u32[]{:S(2)}) %collective-permute-start.17) | collective-permute-done | bytes 520224 | tf_op jit(solution)/shard_map/ppermute | solution.py:18
  864.6 13.9 %collective-permute-done.18 = bf16[6,2048]{0,1:T(8,128)(2,1)S(1)} collective-permute-done((bf16[6,2048]{0,1:T(8,128)(2,1)S(1)}, bf16[6,2048]{0,1:T(8,128)(2,1)S(1)}, u32[]{:S(2)}, u32[]{:S(2)}) %collective-permute-start.18) | collective-permute-done | bytes 24608 | tf_op jit(solution)/shard_map/ppermute | solution.py:18
  881.7 13.3 collective-permute-done.19
  895.1 62.5 %all-gather.24.cloned.1.call-done = bf16[128,4096]{1,0:T(8,128)(2,1)} async-done(((bf16[128,2048]{1,0:T(8,128)(2,1)}), bf16[128,4096]{1,0:T(8,128)(2,1)}) %all-gather.24.cloned.1.call-update) | async-done | bytes 1048592 | tf_op jit(solution)/shard_map/all_gather | solution.py:128
  963.2 14.7 %collective-permute-done.20 = bf16[127,2048]{0,1:T(8,128)(2,1)S(1)} collective-permute-done((bf16[127,2048]{0,1:T(8,128)(2,1)S(1)}, bf16[127,2048]{0,1:T(8,128)(2,1)S(1)}, u32[]{:S(2)}, u32[]{:S(2)}) %collective-permute-start.20) | collective-permute-done | bytes 520224 | tf_op jit(solution)/shard_map/ppermute | solution.py:18
  995.6 13.9 %collective-permute-done.21 = bf16[6,2048]{0,1:T(8,128)(2,1)S(1)} collective-permute-done((bf16[6,2048]{0,1:T(8,128)(2,1)S(1)}, bf16[6,2048]{0,1:T(8,128)(2,1)S(1)}, u32[]{:S(2)}, u32[]{:S(2)}) %collective-permute-start.21) | collective-permute-done | bytes 24608 | tf_op jit(solution)/shard_map/ppermute | solution.py:18
  1012.8 58.8 %collective-permute-done.22 = bf16[128,2048]{1,0:T(8,128)(2,1)} collective-permute-done((bf16[128,2048]{1,0:T(8,128)(2,1)}, bf16[128,2048]{1,0:T(8,128)(2,1)}, u32[]{:S(2)}, u32[]{:S(2)}) %collective-permute-start.22) | collective-permute-done | bytes 524320 | tf_op jit(solution)/shard_map/ppermute | solution.py:18
  1071.7 16.0 %all-gather.26.cloned.1.call-done = bf16[128,4096]{1,0:T(8,128)(2,1)} async-done(((bf16[128,2048]{1,0:T(8,128)(2,1)}), bf16[128,4096]{1,0:T(8,128)(2,1)}) %all-gather.26.cloned.1.call-update) | async-done | bytes 1048592 | tf_op jit(solution)/shard_map/all_gather | solution.py:128
  1087.7 17.5 %conditional.45 = (f32[128,2048]{1,0:T(8,128)}, f32[128,2048]{0,1:T(8,128)}, bf16[128,2048]{0,1:T(8,128)(2,1)}) conditional(s32[]{:T(128)} %convert_element_type.303, () %tuple.260, (bf16[128,4096]{1,0:T(8,128)(2,1)}, bf16[2048,4096]{1,0:T(8,128)(2,1)}) %tuple.655), branch_computations={%region_134.135_spmd, %region_135.136_spmd} | conditional | flops 2148007936 | bytes 22020120 | solution.py:129
  1127.8 15.1 %conditional.46 = (f32[3,128,2048]{1,2,0:T(8,128)}, f32[128,2048]{0,1:T(8,128)}) conditional(s32[]{:T(128)} %convert_element_type.303, () %tuple.259, (f32[128,2048]{1,0:T(8,128)}, f32[128,2048]{0,1:T(8,128)}, bf16[256,2048]{0,1:T(8,128)(2,1)S(1)}, bf16[128,256,128]{2,1,0:T(8,128)(2,1)}, f32[3,128,2048]{1,2,0:T(8,128)S(1)}) %tuple.663), branch_computations={%region_136.137_spmd, %region_137.138_spmd} | conditional | flops 136577024 | bytes 35651656 | solution.py:164
  1175.5 17.8 %copy.335 = f32[128,128,256]{0,2,1:T(8,128)} copy(f32[128,128,256]{2,1,0:T(8,128)} %fusion.30) | data formatting | bytes 33554432 | tf_op jit(solution)/shard_map/reshape | solution.py:37
  1193.4 13.4 %pad.28 = f32[128,32896]{0,1:T(8,128)} pad(f32[128,32768]{0,1:T(8,128)} %bitcast.370, f32[]{:T(128)} %constant.124.clone.1), padding=0_0x0_128 | pad | bytes 33619972 | tf_op jit(solution)/shard_map/jit(_pad)/pad | solution.py:38
  1206.7 17.5 %reshape.320 = f32[128,128,257]{0,2,1:T(8,128)} reshape(f32[128,32896]{0,1:T(8,128)} %pad.28) | data formatting | bytes 33685504 | tf_op jit(solution)/shard_map/reshape | solution.py:39
  1231.0 76.7 %psum.7 = bf16[1,128,128]{1,2,0:T(8,128)(2,1)S(1)} all-reduce(bf16[1,128,128]{1,2,0:T(8,128)(2,1)S(1)} %bitcast.398), channel_id=1, replica_groups=mesh['pipe'=8,'seq'=16,'tp'=2] {'seq'}, use_global_device_ids=true, to_apply=%region_162.163 | all-reduce | flops 16384 | bytes 65536 | tf_op jit(solution)/shard_map/psum | solution.py:219
  (304 shorter events, 484.0 us)
Async XLA Ops:
  7.2 80.0 %all-gather.12.cloned.1.call-start = ((), (), s32[]{:S(2)}) async-start(), calls=%async_computation.1 | async-start | bytes 1572864 | tf_op jit(solution)/shard_map/all_gather | solution.py:128
  7.9 147.3 %all-gather.30.cloned.1.call-start = ((), (), s32[]{:S(2)}) async-start(), calls=%async_computation.10 | async-start | bytes 17825792 | tf_op jit(solution)/shard_map/all_gather | solution.py:194
  8.7 282.8 %all-gather.14.cloned.1.call-start = ((), (), s32[]{:S(2)}) async-start(), calls=%async_computation.2 | async-start | bytes 1572864 | tf_op jit(solution)/shard_map/all_gather | solution.py:128
  14.5 46.4 %collective-permute-start = (bf16[6,2048]{1,0:T(8,128)(2,1)S(1)}, bf16[6,2048]{1,0:T(8,128)(2,1)S(1)}, u32[]{:S(2)}, u32[]{:S(2)}) collective-permute-start(bf16[6,2048]{1,0:T(8,128)(2,1)S(1)} %slice.757), channel_id=1, source_target_pairs={{0,2},{2,4},{4,6},{6,8},{8,10},{10,12},{12,14},{14,16},{16,18},{18... | collective-permute-start | bytes 73736 | tf_op jit(solution)/shard_map/ppermute | solution.py:18
  166.3 14.7 %collective-permute-start.2 = (bf16[127,2048]{0,1:T(8,128)(2,1)}, bf16[127,2048]{0,1:T(8,128)(2,1)}, u32[]{:S(2)}, u32[]{:S(2)}) collective-permute-start(bf16[127,2048]{0,1:T(8,128)(2,1)} %bitcast.344), channel_id=1, source_target_pairs={{2,0},{4,2},{6,4},{8,6},{10,8},{12,10},{14,12},{16,14},{18,16},{20... | collective-permute-start | bytes 1560584 | tf_op jit(solution)/shard_map/ppermute | solution.py:18
  234.5 190.1 %all-gather.16.cloned.1.call-start = ((), (), s32[]{:S(2)}) async-start(), calls=%async_computation.3 | async-start | bytes 1572864 | tf_op jit(solution)/shard_map/all_gather | solution.py:128
  296.2 16.0 %collective-permute-start.5 = (bf16[127,2048]{0,1:T(8,128)(2,1)S(1)}, bf16[127,2048]{0,1:T(8,128)(2,1)S(1)}, u32[]{:S(2)}, u32[]{:S(2)}) collective-permute-start(bf16[127,2048]{0,1:T(8,128)(2,1)S(1)} %bitcast.392), channel_id=1, source_target_pairs={{2,0},{4,2},{6,4},{8,6},{10,8},{12,10},{14,12},{16,14},{18,16},{20... | collective-permute-start | bytes 1560584 | tf_op jit(solution)/shard_map/ppermute | solution.py:18
  328.5 15.2 %collective-permute-start.6 = (bf16[6,2048]{0,1:T(8,128)(2,1)S(1)}, bf16[6,2048]{0,1:T(8,128)(2,1)S(1)}, u32[]{:S(2)}, u32[]{:S(2)}) collective-permute-start(bf16[6,2048]{0,1:T(8,128)(2,1)S(1)} %add_convert_fusion.14), channel_id=1, source_target_pairs={{2,0},{4,2},{6,4},{8,6},{10,8},{12,10},{14,12},{16,14},{18,16},{20... | collective-permute-start | bytes 73736 | tf_op jit(solution)/shard_map/ppermute | solution.py:18
  345.9 14.6 %collective-permute-start.7 = (bf16[128,2048]{1,0:T(8,128)(2,1)}, bf16[128,2048]{1,0:T(8,128)(2,1)}, u32[]{:S(2)}, u32[]{:S(2)}) collective-permute-start(bf16[128,2048]{1,0:T(8,128)(2,1)} %get-tuple-element.1163), channel_id=1, source_target_pairs={{32,0},{64,32},{96,64},{128,96},{160,128},{192,160},{224,192},{33,... | collective-permute-start | bytes 1572872 | tf_op jit(solution)/shard_map/ppermute | solution.py:18
  360.5 197.7 %all-gather.18.cloned.1.call-start = ((), (), s32[]{:S(2)}) async-start(), calls=%async_computation.4 | async-start | bytes 1572864 | tf_op jit(solution)/shard_map/all_gather | solution.py:128
  429.0 16.0 %collective-permute-start.8 = (bf16[127,2048]{0,1:T(8,128)(2,1)S(1)}, bf16[127,2048]{0,1:T(8,128)(2,1)S(1)}, u32[]{:S(2)}, u32[]{:S(2)}) collective-permute-start(bf16[127,2048]{0,1:T(8,128)(2,1)S(1)} %bitcast.393), channel_id=1, source_target_pairs={{2,0},{4,2},{6,4},{8,6},{10,8},{12,10},{14,12},{16,14},{18,16},{20... | collective-permute-start | bytes 1560584 | tf_op jit(solution)/shard_map/ppermute | solution.py:18
  461.5 15.2 %collective-permute-start.9 = (bf16[6,2048]{0,1:T(8,128)(2,1)S(1)}, bf16[6,2048]{0,1:T(8,128)(2,1)S(1)}, u32[]{:S(2)}, u32[]{:S(2)}) collective-permute-start(bf16[6,2048]{0,1:T(8,128)(2,1)S(1)} %add_convert_fusion.13), channel_id=1, source_target_pairs={{2,0},{4,2},{6,4},{8,6},{10,8},{12,10},{14,12},{16,14},{18,16},{20... | collective-permute-start | bytes 73736 | tf_op jit(solution)/shard_map/ppermute | solution.py:18
  478.6 14.6 %collective-permute-start.10 = (bf16[128,2048]{1,0:T(8,128)(2,1)}, bf16[128,2048]{1,0:T(8,128)(2,1)}, u32[]{:S(2)}, u32[]{:S(2)}) collective-permute-start(bf16[128,2048]{1,0:T(8,128)(2,1)} %get-tuple-element.1164), channel_id=1, source_target_pairs={{32,0},{64,32},{96,64},{128,96},{160,128},{192,160},{224,192},{33,... | collective-permute-start | bytes 1572872 | tf_op jit(solution)/shard_map/ppermute | solution.py:18
  493.2 199.5 %all-gather.20.cloned.1.call-start = ((), (), s32[]{:S(2)}) async-start(), calls=%async_computation.5 | async-start | bytes 1572864 | tf_op jit(solution)/shard_map/all_gather | solution.py:128
  562.5 16.0 %collective-permute-start.11 = (bf16[127,2048]{0,1:T(8,128)(2,1)S(1)}, bf16[127,2048]{0,1:T(8,128)(2,1)S(1)}, u32[]{:S(2)}, u32[]{:S(2)}) collective-permute-start(bf16[127,2048]{0,1:T(8,128)(2,1)S(1)} %bitcast.394), channel_id=1, source_target_pairs={{2,0},{4,2},{6,4},{8,6},{10,8},{12,10},{14,12},{16,14},{18,16},{20... | collective-permute-start | bytes 1560584 | tf_op jit(solution)/shard_map/ppermute | solution.py:18
  595.2 15.2 %collective-permute-start.12 = (bf16[6,2048]{0,1:T(8,128)(2,1)S(1)}, bf16[6,2048]{0,1:T(8,128)(2,1)S(1)}, u32[]{:S(2)}, u32[]{:S(2)}) collective-permute-start(bf16[6,2048]{0,1:T(8,128)(2,1)S(1)} %add_convert_fusion.12), channel_id=1, source_target_pairs={{2,0},{4,2},{6,4},{8,6},{10,8},{12,10},{14,12},{16,14},{18,16},{20... | collective-permute-start | bytes 73736 | tf_op jit(solution)/shard_map/ppermute | solution.py:18
  612.4 14.6 %collective-permute-start.13 = (bf16[128,2048]{1,0:T(8,128)(2,1)}, bf16[128,2048]{1,0:T(8,128)(2,1)}, u32[]{:S(2)}, u32[]{:S(2)}) collective-permute-start(bf16[128,2048]{1,0:T(8,128)(2,1)} %get-tuple-element.1165), channel_id=1, source_target_pairs={{32,0},{64,32},{96,64},{128,96},{160,128},{192,160},{224,192},{33,... | collective-permute-start | bytes 1572872 | tf_op jit(solution)/shard_map/ppermute | solution.py:18
  627.0 199.2 %all-gather.22.cloned.1.call-start = ((), (), s32[]{:S(2)}) async-start(), calls=%async_computation.6 | async-start | bytes 1572864 | tf_op jit(solution)/shard_map/all_gather | solution.py:128
  697.2 16.0 %collective-permute-start.14 = (bf16[127,2048]{0,1:T(8,128)(2,1)S(1)}, bf16[127,2048]{0,1:T(8,128)(2,1)S(1)}, u32[]{:S(2)}, u32[]{:S(2)}) collective-permute-start(bf16[127,2048]{0,1:T(8,128)(2,1)S(1)} %bitcast.395), channel_id=1, source_target_pairs={{2,0},{4,2},{6,4},{8,6},{10,8},{12,10},{14,12},{16,14},{18,16},{20... | collective-permute-start | bytes 1560584 | tf_op jit(solution)/shard_map/ppermute | solution.py:18
  729.6 15.2 %collective-permute-start.15 = (bf16[6,2048]{0,1:T(8,128)(2,1)S(1)}, bf16[6,2048]{0,1:T(8,128)(2,1)S(1)}, u32[]{:S(2)}, u32[]{:S(2)}) collective-permute-start(bf16[6,2048]{0,1:T(8,128)(2,1)S(1)} %add_convert_fusion.11), channel_id=1, source_target_pairs={{2,0},{4,2},{6,4},{8,6},{10,8},{12,10},{14,12},{16,14},{18,16},{20... | collective-permute-start | bytes 73736 | tf_op jit(solution)/shard_map/ppermute | solution.py:18
  746.9 14.6 %collective-permute-start.16 = (bf16[128,2048]{1,0:T(8,128)(2,1)}, bf16[128,2048]{1,0:T(8,128)(2,1)}, u32[]{:S(2)}, u32[]{:S(2)}) collective-permute-start(bf16[128,2048]{1,0:T(8,128)(2,1)} %get-tuple-element.1166), channel_id=1, source_target_pairs={{32,0},{64,32},{96,64},{128,96},{160,128},{192,160},{224,192},{33,... | collective-permute-start | bytes 1572872 | tf_op jit(solution)/shard_map/ppermute | solution.py:18
  761.5 196.0 %all-gather.24.cloned.1.call-start = ((), (), s32[]{:S(2)}) async-start(), calls=%async_computation.7 | async-start | bytes 1572864 | tf_op jit(solution)/shard_map/all_gather | solution.py:128
  830.6 16.0 %collective-permute-start.17 = (bf16[127,2048]{0,1:T(8,128)(2,1)S(1)}, bf16[127,2048]{0,1:T(8,128)(2,1)S(1)}, u32[]{:S(2)}, u32[]{:S(2)}) collective-permute-start(bf16[127,2048]{0,1:T(8,128)(2,1)S(1)} %bitcast.396), channel_id=1, source_target_pairs={{2,0},{4,2},{6,4},{8,6},{10,8},{12,10},{14,12},{16,14},{18,16},{20... | collective-permute-start | bytes 1560584 | tf_op jit(solution)/shard_map/ppermute | solution.py:18
  863.3 15.2 %collective-permute-start.18 = (bf16[6,2048]{0,1:T(8,128)(2,1)S(1)}, bf16[6,2048]{0,1:T(8,128)(2,1)S(1)}, u32[]{:S(2)}, u32[]{:S(2)}) collective-permute-start(bf16[6,2048]{0,1:T(8,128)(2,1)S(1)} %add_convert_fusion.10), channel_id=1, source_target_pairs={{2,0},{4,2},{6,4},{8,6},{10,8},{12,10},{14,12},{16,14},{18,16},{20... | collective-permute-start | bytes 73736 | tf_op jit(solution)/shard_map/ppermute | solution.py:18
  880.4 14.6 %collective-permute-start.19 = (bf16[128,2048]{1,0:T(8,128)(2,1)}, bf16[128,2048]{1,0:T(8,128)(2,1)}, u32[]{:S(2)}, u32[]{:S(2)}) collective-permute-start(bf16[128,2048]{1,0:T(8,128)(2,1)} %get-tuple-element.1167), channel_id=1, source_target_pairs={{32,0},{64,32},{96,64},{128,96},{160,128},{192,160},{224,192},{33,... | collective-permute-start | bytes 1572872 | tf_op jit(solution)/shard_map/ppermute | solution.py:18
  895.0 192.6 %all-gather.26.cloned.1.call-start = ((), (), s32[]{:S(2)}) async-start(), calls=%async_computation.8 | async-start | bytes 1572864 | tf_op jit(solution)/shard_map/all_gather | solution.py:128
  961.9 16.0 %collective-permute-start.20 = (bf16[127,2048]{0,1:T(8,128)(2,1)S(1)}, bf16[127,2048]{0,1:T(8,128)(2,1)S(1)}, u32[]{:S(2)}, u32[]{:S(2)}) collective-permute-start(bf16[127,2048]{0,1:T(8,128)(2,1)S(1)} %bitcast.397), channel_id=1, source_target_pairs={{2,0},{4,2},{6,4},{8,6},{10,8},{12,10},{14,12},{16,14},{18,16},{20... | collective-permute-start | bytes 1560584 | tf_op jit(solution)/shard_map/ppermute | solution.py:18
  994.3 15.2 %collective-permute-start.21 = (bf16[6,2048]{0,1:T(8,128)(2,1)S(1)}, bf16[6,2048]{0,1:T(8,128)(2,1)S(1)}, u32[]{:S(2)}, u32[]{:S(2)}) collective-permute-start(bf16[6,2048]{0,1:T(8,128)(2,1)S(1)} %add_convert_fusion.9), channel_id=1, source_target_pairs={{2,0},{4,2},{6,4},{8,6},{10,8},{12,10},{14,12},{16,14},{18,16},{20... | collective-permute-start | bytes 73736 | tf_op jit(solution)/shard_map/ppermute | solution.py:18
  1011.5 60.1 %collective-permute-start.22 = (bf16[128,2048]{1,0:T(8,128)(2,1)}, bf16[128,2048]{1,0:T(8,128)(2,1)}, u32[]{:S(2)}, u32[]{:S(2)}) collective-permute-start(bf16[128,2048]{1,0:T(8,128)(2,1)} %get-tuple-element.1168), channel_id=1, source_target_pairs={{32,0},{64,32},{96,64},{128,96},{160,128},{192,160},{224,192},{33,... | collective-permute-start | bytes 1572872 | tf_op jit(solution)/shard_map/ppermute | solution.py:18
  1071.6 250.9 %all-gather.28.cloned.1.call-start = ((), (), s32[]{:S(2)}) async-start(), calls=%async_computation.9 | async-start | bytes 1671168 | tf_op jit(solution)/shard_map/all_gather | solution.py:9
  1107.9 18.2 %collective-permute-start.23 = (bf16[127,2048]{0,1:T(8,128)(2,1)}, bf16[127,2048]{0,1:T(8,128)(2,1)}, u32[]{:S(2)}, u32[]{:S(2)}) collective-permute-start(bf16[127,2048]{0,1:T(8,128)(2,1)} %bitcast.351), channel_id=1, source_target_pairs={{2,0},{4,2},{6,4},{8,6},{10,8},{12,10},{14,12},{16,14},{18,16},{20... | collective-permute-start | bytes 1560584 | tf_op jit(solution)/shard_map/ppermute | solution.py:18
  1166.0 142.4 %collective-permute-start.24 = (bf16[6,2048]{0,1:T(8,128)(2,1)S(1)}, bf16[6,2048]{0,1:T(8,128)(2,1)S(1)}, u32[]{:S(2)}, u32[]{:S(2)}) collective-permute-start(bf16[6,2048]{0,1:T(8,128)(2,1)S(1)} %add_convert_fusion.8), channel_id=1, source_target_pairs={{2,0},{4,2},{6,4},{8,6},{10,8},{12,10},{14,12},{16,14},{18,16},{20... | collective-permute-start | bytes 73736 | tf_op jit(solution)/shard_map/ppermute | solution.py:18
  (34 other events, 149.2 us)
Sparse Core Ops, SparseCore 0:
  9.8 15.8 all-gather.11
  28.1 127.0 all-gather.29
  234.6 56.8 all-gather.13
  360.6 63.8 all-gather.15
  493.4 64.7 all-gather.17
  627.1 65.5 all-gather.19
  761.6 64.5 all-gather.21
  895.1 62.3 all-gather.23
  1071.7 15.8 all-gather.25
  1153.8 50.0 all-gather.27
